TPU v7x, 32 devices: a whole 2x2x4 slice. The times are simulated.
32 devices in a mesh: row: 8 (over y, x, core), rep: 4 (over z).
Axes of the slice: x: 2, y: 2, z: 4, core: 2. Of those that a mesh axis runs over, the one named last changes fastest.
Arguments:
- features: bfloat16 [8192, 256], P('row'), may hold values from -6 to 6
- weight_self: bfloat16 [256, 256], replicated, may hold values from -0.375 to 0.375
- weight_neigh: bfloat16 [256, 256], replicated, may hold values from -0.375 to 0.375
- degrees: int32 [8192], P('row'), may hold values from 1 to 47
- tile_values: bfloat16 [8, 8, 48, 128, 128], P('row', 'rep'), may hold values from 0 to 1
- tile_blocks: int32 [8, 8, 48, 2], P('row', 'rep'), may hold values from 0 to 7
- tile_count: int32 [8, 8], P('row', 'rep'), may hold values from 1 to 48, as said below
- cotangent: bfloat16 [8192, 256], P(('row', 'rep')), may hold values from -6 to 6
Outputs:
- output: bfloat16 [8192, 256], P(('row', 'rep'))
- grad_self: float32 [256, 256], replicated
- grad_neigh: float32 [256, 256], replicated
- grad_features: bfloat16 [8192, 256], P(('row', 'rep'))
Inputs may be any that keep to these rules, and one draw needn't show every extreme that they name: `tile_count`: for some row index and section all 48 slots are live in every draw.
All inputs are finite; a program needn't handle non-finite values.
Results may differ from a plain program's by a relative error of at most 0.024.
Values may be sent and summed in bfloat16 or wider, within the bound.
A program may use at most 64 MiB of HBM per device.

v0:
```python
import jax
import jax.numpy as jnp
from jax import lax
from jax.sharding import PartitionSpec as P


def from_root(value, axis, source):
    kept = jnp.where(lax.axis_index(axis) == source, value, 0).astype(value.dtype)
    return lax.psum(kept, axis)


def hot_tables(blocks, count, nblk, slots):
    live = (jnp.arange(slots) < count).astype(jnp.float32)
    dest_hot = (blocks[:, 0][:, None] == jnp.arange(nblk)[None, :]).astype(jnp.float32) * live[
        :, None
    ]
    src_hot = (blocks[:, 1][:, None] == jnp.arange(nblk)[None, :]).astype(jnp.float32)
    return (dest_hot, src_hot)


def body(
    features, weight_self, weight_neigh, degrees, tile_values, tile_blocks, tile_count, cotangent
):
    rows, width = features.shape
    tile = tile_values.shape[3]
    slots = tile_values.shape[2]
    sections_here = tile_values.shape[1]
    nblk = rows // tile
    nrep = lax.axis_size("rep")
    share = rows // nrep
    rep_pos = lax.axis_index("rep")
    row_pos = lax.axis_index("row")
    partial_value = jnp.zeros((nblk, tile, width), jnp.float32)
    for section in range(sections_here):
        source = from_root(features, "row", rep_pos * sections_here + section)
        source_blocks = source.reshape(nblk, tile, width)
        dest_hot, src_hot = hot_tables(tile_blocks[0, section], tile_count[0, section], nblk, slots)
        picked = jnp.einsum(
            "tc,cif->tif",
            src_hot.astype(jnp.bfloat16),
            source_blocks,
            preferred_element_type=jnp.bfloat16,
        )
        prod = jnp.einsum(
            "tij,tjf->tif", tile_values[0, section], picked, preferred_element_type=jnp.float32
        )
        partial_value = partial_value + jnp.einsum("tb,tif->bif", dest_hot, prod)
    partial_value = partial_value.reshape(rows, width)
    degree_all = degrees.astype(jnp.float32)[:, None]
    degree_mine = lax.dynamic_slice_in_dim(degree_all, rep_pos * share, share, 0)
    feat_mine = lax.dynamic_slice_in_dim(features, rep_pos * share, share, 0)
    agg_part = lax.psum_scatter(partial_value, "rep", scatter_dimension=0, tiled=True)
    agg_mine = (agg_part / degree_mine).astype(jnp.bfloat16)
    pre = jnp.dot(feat_mine, weight_self, preferred_element_type=jnp.float32) + jnp.dot(
        agg_mine, weight_neigh, preferred_element_type=jnp.float32
    )
    sig = jax.nn.sigmoid(pre)
    gpre_mine = (cotangent.astype(jnp.float32) * sig * (1.0 + pre * (1.0 - sig))).astype(
        jnp.bfloat16
    )
    dagg_mine = (
        jnp.dot(gpre_mine, weight_neigh.T, preferred_element_type=jnp.float32) / degree_mine
    ).astype(jnp.bfloat16)
    dagg_all = lax.all_gather(dagg_mine, "rep", axis=0, tiled=True)
    output = jax.nn.silu(pre).astype(jnp.bfloat16)
    grad_self_part = jnp.dot(feat_mine.T, gpre_mine, preferred_element_type=jnp.float32)
    grad_neigh_part = jnp.dot(agg_mine.T, gpre_mine, preferred_element_type=jnp.float32)
    grad_self, grad_neigh = lax.psum((grad_self_part, grad_neigh_part), ("row", "rep"))
    dagg_blocks = dagg_all.reshape(nblk, tile, width)
    terms = []
    for section in range(sections_here):
        dest_hot, src_hot = hot_tables(tile_blocks[0, section], tile_count[0, section], nblk, slots)
        picked = jnp.einsum(
            "tb,bif->tif",
            dest_hot.astype(jnp.bfloat16),
            dagg_blocks,
            preferred_element_type=jnp.bfloat16,
        )
        contrib = jnp.einsum(
            "tij,tif->tjf", tile_values[0, section], picked, preferred_element_type=jnp.float32
        )
        terms.append(jnp.einsum("tc,tjf->cjf", src_hot, contrib).reshape(rows, width))
    stacked = jnp.stack(terms, 0)
    summed = lax.psum(stacked, "row")
    owned = lax.dynamic_index_in_dim(summed, row_pos % sections_here, 0, keepdims=False).astype(
        jnp.bfloat16
    )
    everyone = from_root(owned, "rep", row_pos // sections_here)
    back_mine = lax.dynamic_slice_in_dim(everyone, rep_pos * share, share, 0)
    grad_features = (
        jnp.dot(gpre_mine, weight_self.T, preferred_element_type=jnp.float32)
        + back_mine.astype(jnp.float32)
    ).astype(jnp.bfloat16)
    return (output, grad_self, grad_neigh, grad_features)


def solution(mesh):
    in_specs = (
        P("row", None),
        P(),
        P(),
        P("row"),
        P("row", "rep", None, None, None),
        P("row", "rep", None, None),
        P("row", "rep"),
        P(("row", "rep"), None),
    )
    out_specs = (P(("row", "rep"), None), P(), P(), P(("row", "rep"), None))
    return jax.shard_map(body, mesh=mesh, in_specs=in_specs, out_specs=out_specs, check_vma=False)
```

profile of v0, /device:TPU:0, one launch (start us, length us, event | category | flops | bytes accessed | tf_op | source)
XLA Modules:
  0.0 399.4 jit_solution(14081113110862203722)
XLA Ops:
  7.2 2.3 broadcast_select_fusion.1
  13.0 57.8 %all-reduce.11.cloned.1.call-done = (bf16[8,128,256]{2,1,0:T(8,128)(2,1)}, bf16[8,128,256]{2,1,0:T(8,128)(2,1)}) async-done(((bf16[8,128,256]{2,1,0:T(8,128)(2,1)}, bf16[8,128,256]{2,1,0:T(8,128)(2,1)}), (bf16[8,128,256]{2,1,0:T(8,128)(2,1)}, bf16[8,128,256]{2,1,0:T(8,128)(2,1)})) %all-reduce.11.cloned.1.call-update) | async-done | bytes 1048592 | tf_op jit(solution)/shard_map/psum | solution.py:9
  70.7 2.1 fusion.31
  72.8 3.3 fusion.12
  76.0 3.8 copy.22
  79.9 2.2 fusion.33
  82.1 3.2 fusion.14
  85.3 4.9 %copy.19 = bf16[48,256,128]{1,0,2:T(8,128)(2,1)} copy(bf16[48,256,128]{2,1,0:T(8,128)(2,1)} %fusion.14) | data formatting | bytes 6291456 | tf_op jit(solution)/shard_map/tij,tjf->tif/dot_general | solution.py:44
  95.3 25.4 %reduce-scatter.2.cloned.1.call-done = f32[256,256]{1,0:T(8,128)} async-done(((f32[1024,256]{1,0:T(8,128)}), f32[256,256]{1,0:T(8,128)}) %reduce-scatter.2.cloned.1.call-update) | async-done | bytes 262160 | tf_op jit(solution)/shard_map/reduce_scatter | solution.py:52
  120.7 1.9 multiply_convert_fusion
  122.9 16.2 %all_gather.3 = bf16[1024,256]{1,0:T(8,128)(2,1)S(1)} all-gather(bf16[256,256]{1,0:T(8,128)(2,1)S(1)} %fusion.28), channel_id=1, replica_groups=mesh['row'=8,'rep'=4] {'rep'}, dimensions={0}, use_global_device_ids=true | all-gather | bytes 655360 | tf_op jit(solution)/shard_map/all_gather | solution.py:64
  140.1 2.7 fusion.35
  142.8 3.1 fusion.10
  145.9 3.8 copy.25
  153.0 3.1 fusion.8
  156.1 3.8 copy.27
  161.3 56.4 %all-reduce.12 = bf16[2,1024,256]{2,1,0:T(8,128)(2,1)S(1)} all-reduce(f32[2,1024,256]{2,1,0:T(8,128)S(1)} %pad_maximum_fusion), channel_id=1, replica_groups=mesh['row'=8,'rep'=4] {'row'}, use_global_device_ids=true, to_apply=%region_5.6 | all-reduce | flops 524288 | bytes 3145728 | tf_op jit(solution)/shard_map/psum | solution.py:84
  218.6 1.8 fusion.39
  220.4 2.0 fusion.77
  222.4 32.1 %all-reduce.7.cloned.1.call-done = bf16[1024,256]{1,0:T(8,128)(2,1)} async-done(((bf16[1024,256]{1,0:T(8,128)(2,1)}), bf16[1024,256]{1,0:T(8,128)(2,1)}) %all-reduce.7.cloned.1.call-update) | async-done | bytes 524304 | tf_op jit(solution)/shard_map/psum | solution.py:9
  254.5 1.8 fusion.27
  256.3 133.3 %all-reduce.9.cloned.1.call-done = (f32[256,256]{1,0:T(8,128)}, f32[256,256]{1,0:T(8,128)}) async-done(((f32[256,256]{1,0:T(8,128)}, f32[256,256]{1,0:T(8,128)}), (f32[256,256]{1,0:T(8,128)}, f32[256,256]{1,0:T(8,128)})) %all-reduce.9.cloned.1.call-update) | async-done | bytes 524304 | tf_op jit(solution)/shard_map/psum | solution.py:68
  389.6 1.7 copy.51
  391.2 1.7 copy.52
  (61 shorter events, 15.1 us)
Async XLA Ops:
  7.2 113.6 %copy-start = (bf16[256,256]{1,0:T(8,128)(2,1)S(1)}, bf16[256,256]{1,0:T(8,128)(2,1)}, u32[]{:S(2)}) copy-start(bf16[256,256]{1,0:T(8,128)(2,1)} %param.10) | copy-start | bytes 393220
  7.2 63.5 %all-reduce.11.cloned.1.call-start = ((), (), s32[]{:S(2)}) async-start(), calls=%async_computation.4 | async-start | bytes 2097152 | tf_op jit(solution)/shard_map/psum | solution.py:9
  7.2 65.5 %copy-start.3 = (bf16[1,2,48,128,128]{4,3,2,1,0:T(8,128)(2,1)S(1)}, bf16[1,2,48,128,128]{4,3,2,1,0:T(8,128)(2,1)}, u32[]{:S(2)}) copy-start(bf16[1,2,48,128,128]{4,3,2,1,0:T(8,128)(2,1)} %param.12) | copy-start | bytes 9437188
  9.5 111.2 %reduce-scatter.2.cloned.1.call-start = ((), (), s32[]{:S(2)}) async-start(), calls=%async_computation.1 | async-start | bytes 1310720 | tf_op jit(solution)/shard_map/reduce_scatter | solution.py:52
  11.6 78.7 %copy-start.10 = (bf16[48]{0:T(256)(128)(2,1)}, bf16[48]{0:T(256)(128)(2,1)S(1)}, u32[]{:S(2)}) copy-start(bf16[48]{0:T(256)(128)(2,1)S(1)} %compare_convert_fusion) | copy-start | bytes 292
  12.2 78.5 %copy-start.12 = (bf16[48]{0:T(256)(128)(2,1)}, bf16[48]{0:T(256)(128)(2,1)S(1)}, u32[]{:S(2)}) copy-start(bf16[48]{0:T(256)(128)(2,1)S(1)} %compare_convert_fusion.1) | copy-start | bytes 292
  79.9 2.2 copy-start.4
  90.2 1.9 copy-start.1
  92.1 1.9 copy-start.9
  92.1 2.1 copy-start.8
  92.7 28.1 %copy-start.16 = (bf16[256,256]{1,0:T(8,128)(2,1)S(1)}, bf16[256,256]{1,0:T(8,128)(2,1)}, u32[]{:S(2)}) copy-start(bf16[256,256]{1,0:T(8,128)(2,1)} %param.15) | copy-start | bytes 393220
  94.0 45.1 %copy-start.13 = (bf16[48]{0:T(256)(128)(2,1)S(1)}, bf16[48]{0:T(256)(128)(2,1)}, u32[]{:S(2)}) copy-start(bf16[48]{0:T(256)(128)(2,1)} %copy-done.12) | copy-start | bytes 292
  94.0 160.5 %all-reduce.7.cloned.1.call-start = ((), (), s32[]{:S(2)}) async-start(), calls=%async_computation.2 | async-start | bytes 1048576 | tf_op jit(solution)/shard_map/psum | solution.py:9
  94.2 45.9 %copy-start.14 = (f32[256]{0:T(256)}, f32[256]{0:T(256)S(1)}, u32[]{:S(2)}) copy-start(f32[256]{0:T(256)S(1)} %dynamic-slice.3) | copy-start | bytes 3076
  122.7 17.5 %copy-start.11 = (bf16[48]{0:T(256)(128)(2,1)S(1)}, bf16[48]{0:T(256)(128)(2,1)}, u32[]{:S(2)}) copy-start(bf16[48]{0:T(256)(128)(2,1)} %copy-done.10) | copy-start | bytes 292
  139.1 3.7 copy-start.5
  149.8 2.1 copy-start.2
  149.8 3.2 copy-start.6
  159.9 1.2 copy-start.7
  161.3 59.1 %copy-start.15 = (f32[256]{0:T(256)S(1)}, f32[256]{0:T(256)}, u32[]{:S(2)}) copy-start(f32[256]{0:T(256)} %copy-done.14) | copy-start | bytes 3076
  218.5 171.0 %all-reduce.9.cloned.1.call-start = ((), (), s32[]{:S(2)}) async-start(), calls=%async_computation.3 | async-start | bytes 1048576 | tf_op jit(solution)/shard_map/psum | solution.py:68
Sparse Core Ops, SparseCore 0:
  11.2 59.4 all-reduce.10
  94.1 26.5 reduce-scatter.1
  218.7 35.8 all-reduce.6
  260.4 129.1 all-reduce.8
where the time goes:
time: 400 us; the launch traced here: 399 us
  waiting for transfers between devices  249 us (62%)
  blocking collectives  72.6 us (18%)
  matrix products  31.5 us (8%)
  local copies, waits for them, and re-layouts  28 us (7%)
  between operations  14 us (4%)
  other arithmetic  4.54 us (1%)
    psum x1, waiting for transfers between devices, body(): lax.psum((grad_self_part, grad_neigh_part), ('row', 'rep'))  133 us
    psum x2, waiting for transfers between devices, from_root(): return lax.psum(kept, axis)  89.8 us
    psum x1, blocking collectives, body(): summed = lax.psum(stacked, 'row')  56.4 us
    reduce_scatter x1, waiting for transfers between devices, body(): lax.psum_scatter(partial_value, 'rep', scatter_dimension=0, tiled=True)  25.4 us
    all_gather x1, blocking collectives, body(): dagg_all = lax.all_gather(dagg_mine, 'rep', axis=0, tiled=True)  16.2 us
    dot_general x2, local copies, waits for them, and re-layouts, body(): jnp.einsum('tij,tjf->tif', tile_values[0, section], picked, preferred_ele...  8.77 us
  transfers between devices with their start and end apart: 4, of which 4 were waited for; matrix products, arithmetic and copies ran while one was open for 3% of the time, Pallas kernels for 0%

commit v1 on v0

--- a/solution.py
+++ b/solution.py
@@ -2,6 +2,15 @@
 import jax.numpy as jnp
 from jax import lax
 from jax.sharding import PartitionSpec as P
+
+
+def added_up(shard, mesh_axis):
+    size = lax.axis_size(mesh_axis)
+    total, hop = (shard, 1)
+    while hop < size:
+        total = total + lax.ppermute(total, mesh_axis, [(i, i ^ hop) for i in range(size)])
+        hop = 2 * hop
+    return total
 
 
 def from_root(value, axis, source):
@@ -81,7 +90,7 @@
         )
         terms.append(jnp.einsum("tc,tjf->cjf", src_hot, contrib).reshape(rows, width))
     stacked = jnp.stack(terms, 0)
-    summed = lax.psum(stacked, "row")
+    summed = added_up(stacked, "row")
     owned = lax.dynamic_index_in_dim(summed, row_pos % sections_here, 0, keepdims=False).astype(
         jnp.bfloat16
     )

time: 400 us -> 448 us (1.12)
  waiting for transfers between devices: 249 us -> 346 us
  blocking collectives: 72.6 us -> 16.2 us
    ppermute x0 -> x3, waiting for transfers between devices: none -> 95.8 us  [added_up(): lax.ppermute(total, mesh_axis, [(i, i ^ hop) for i in range(size)])]
    psum x1 -> x0, blocking collectives: 56.4 us -> none  [body(): summed = lax.psum(stacked, 'row')]
  transfers between devices with their start and end apart: 4 -> 7, of which waited for: 4 -> 7; matrix products, arithmetic and copies ran while one was open for 3% -> 2% of each run, Pallas kernels for 0% -> 0%
where the time goes in v1:
time: 448 us; the launch traced here: 447 us
  waiting for transfers between devices  346 us (77%)
  matrix products  32.4 us (7%)
  local copies, waits for them, and re-layouts  28.5 us (6%)
  blocking collectives  16.2 us (4%)
  between operations  14 us (3%)
  other arithmetic  6.6 us (1%)
    psum x1, waiting for transfers between devices, body(): lax.psum((grad_self_part, grad_neigh_part), ('row', 'rep'))  133 us
    ppermute x3, waiting for transfers between devices, added_up(): lax.ppermute(total, mesh_axis, [(i, i ^ hop) for i in range(size)])  95.8 us
    psum x2, waiting for transfers between devices, from_root(): return lax.psum(kept, axis)  91.9 us
    reduce_scatter x1, waiting for transfers between devices, body(): lax.psum_scatter(partial_value, 'rep', scatter_dimension=0, tiled=True)  25.5 us
    all_gather x1, blocking collectives, body(): dagg_all = lax.all_gather(dagg_mine, 'rep', axis=0, tiled=True)  16.2 us
  transfers between devices with their start and end apart: 7, of which 7 were waited for; matrix products, arithmetic and copies ran while one was open for 2% of the time, Pallas kernels for 0%

profile of v1, /device:TPU:0, one launch (start us, length us, event | category | flops | bytes accessed | tf_op | source)
XLA Modules:
  0.0 447.4 jit_solution(16339874532167293085)
XLA Ops:
  7.3 2.3 broadcast_select_fusion.1
  13.0 57.7 %all-reduce.10.cloned.1.call-done = (bf16[8,128,256]{2,1,0:T(8,128)(2,1)}, bf16[8,128,256]{2,1,0:T(8,128)(2,1)}) async-done(((bf16[8,128,256]{2,1,0:T(8,128)(2,1)}, bf16[8,128,256]{2,1,0:T(8,128)(2,1)}), (bf16[8,128,256]{2,1,0:T(8,128)(2,1)}, bf16[8,128,256]{2,1,0:T(8,128)(2,1)})) %all-reduce.10.cloned.1.call-update) | async-done | bytes 1048592 | tf_op jit(solution)/shard_map/psum | solution.py:18
  70.7 2.1 fusion.32
  72.8 3.2 fusion.12
  76.0 3.8 copy.22
  79.9 2.2 fusion.34
  82.1 3.2 fusion.14
  85.3 5.0 %copy.19 = bf16[48,256,128]{1,0,2:T(8,128)(2,1)} copy(bf16[48,256,128]{2,1,0:T(8,128)(2,1)} %fusion.14) | data formatting | bytes 6291456 | tf_op jit(solution)/shard_map/tij,tjf->tif/dot_general | solution.py:53
  95.3 25.5 %reduce-scatter.2.cloned.1.call-done = f32[256,256]{1,0:T(8,128)} async-done(((f32[1024,256]{1,0:T(8,128)}), f32[256,256]{1,0:T(8,128)}) %reduce-scatter.2.cloned.1.call-update) | async-done | bytes 262160 | tf_op jit(solution)/shard_map/reduce_scatter | solution.py:61
  120.7 1.9 multiply_convert_fusion
  122.9 16.2 %all_gather.3 = bf16[1024,256]{1,0:T(8,128)(2,1)S(1)} all-gather(bf16[256,256]{1,0:T(8,128)(2,1)S(1)} %fusion.28), channel_id=1, replica_groups=mesh['row'=8,'rep'=4] {'rep'}, dimensions={0}, use_global_device_ids=true | all-gather | bytes 655360 | tf_op jit(solution)/shard_map/all_gather | solution.py:73
  140.1 2.6 fusion.36
  142.8 3.1 fusion.10
  145.9 3.8 copy.25
  152.6 3.1 fusion.8
  155.7 5.0 %copy.27 = bf16[48,256,128]{1,0,2:T(8,128)(2,1)} copy(bf16[48,256,128]{2,1,0:T(8,128)(2,1)} %fusion.8) | data formatting | bytes 6291456 | tf_op jit(solution)/shard_map/tij,tif->tjf/dot_general | solution.py:88
  160.6 2.4 fusion
  163.6 4.1 collective-permute-done
  169.5 46.2 %collective-permute-done.1 = f32[2,1024,256]{2,1,0:T(8,128)S(1)} collective-permute-done((f32[2,1024,256]{2,1,0:T(8,128)S(1)}, f32[2,1024,256]{2,1,0:T(8,128)S(1)}, u32[]{:S(2)}, u32[]{:S(2)}) %collective-permute-start.1) | collective-permute-done | bytes 2097184 | tf_op jit(solution)/shard_map/ppermute | solution.py:11
  217.8 45.4 %collective-permute-done.2 = f32[2,1024,256]{2,1,0:T(8,128)} collective-permute-done((f32[2,1024,256]{2,1,0:T(8,128)S(1)}, f32[2,1024,256]{2,1,0:T(8,128)}, u32[]{:S(2)}, u32[]{:S(2)}) %collective-permute-start.2) | collective-permute-done | bytes 2097184 | tf_op jit(solution)/shard_map/ppermute | solution.py:11
  263.2 2.2 fusion.31
  265.4 1.8 fusion.40
  268.3 34.2 %all-reduce.6.cloned.1.call-done = bf16[1024,256]{1,0:T(8,128)(2,1)} async-done(((bf16[1024,256]{1,0:T(8,128)(2,1)}), bf16[1024,256]{1,0:T(8,128)(2,1)}) %all-reduce.6.cloned.1.call-update) | async-done | bytes 524304 | tf_op jit(solution)/shard_map/psum | solution.py:18
  304.3 133.3 %all-reduce.8.cloned.1.call-done = (f32[256,256]{1,0:T(8,128)}, f32[256,256]{1,0:T(8,128)}) async-done(((f32[256,256]{1,0:T(8,128)}, f32[256,256]{1,0:T(8,128)}), (f32[256,256]{1,0:T(8,128)}, f32[256,256]{1,0:T(8,128)})) %all-reduce.8.cloned.1.call-update) | async-done | bytes 524304 | tf_op jit(solution)/shard_map/psum | solution.py:77
  (70 shorter events, 23.0 us)
Async XLA Ops:
  7.2 113.6 %copy-start = (bf16[256,256]{1,0:T(8,128)(2,1)S(1)}, bf16[256,256]{1,0:T(8,128)(2,1)}, u32[]{:S(2)}) copy-start(bf16[256,256]{1,0:T(8,128)(2,1)} %param.10) | copy-start | bytes 393220
  7.2 63.5 %all-reduce.10.cloned.1.call-start = ((), (), s32[]{:S(2)}) async-start(), calls=%async_computation.4 | async-start | bytes 2097152 | tf_op jit(solution)/shard_map/psum | solution.py:18
  7.2 65.5 %copy-start.4 = (bf16[1,2,48,128,128]{4,3,2,1,0:T(8,128)(2,1)S(1)}, bf16[1,2,48,128,128]{4,3,2,1,0:T(8,128)(2,1)}, u32[]{:S(2)}) copy-start(bf16[1,2,48,128,128]{4,3,2,1,0:T(8,128)(2,1)} %param.12) | copy-start | bytes 9437188
  9.6 111.2 %reduce-scatter.2.cloned.1.call-start = ((), (), s32[]{:S(2)}) async-start(), calls=%async_computation.1 | async-start | bytes 1310720 | tf_op jit(solution)/shard_map/reduce_scatter | solution.py:61
  11.6 78.7 %copy-start.10 = (bf16[48]{0:T(256)(128)(2,1)}, bf16[48]{0:T(256)(128)(2,1)S(1)}, u32[]{:S(2)}) copy-start(bf16[48]{0:T(256)(128)(2,1)S(1)} %compare_convert_fusion) | copy-start | bytes 292
  12.3 78.5 %copy-start.12 = (bf16[48]{0:T(256)(128)(2,1)}, bf16[48]{0:T(256)(128)(2,1)S(1)}, u32[]{:S(2)}) copy-start(bf16[48]{0:T(256)(128)(2,1)S(1)} %compare_convert_fusion.1) | copy-start | bytes 292
  79.9 2.2 copy-start.5
  92.2 1.9 copy-start.9
  92.2 2.0 copy-start.8
  92.7 28.1 %copy-start.17 = (bf16[256,256]{1,0:T(8,128)(2,1)S(1)}, bf16[256,256]{1,0:T(8,128)(2,1)}, u32[]{:S(2)}) copy-start(bf16[256,256]{1,0:T(8,128)(2,1)} %param.15) | copy-start | bytes 393220
  94.0 45.1 %copy-start.13 = (bf16[48]{0:T(256)(128)(2,1)S(1)}, bf16[48]{0:T(256)(128)(2,1)}, u32[]{:S(2)}) copy-start(bf16[48]{0:T(256)(128)(2,1)} %copy-done.12) | copy-start | bytes 292
  94.0 208.5 %all-reduce.6.cloned.1.call-start = ((), (), s32[]{:S(2)}) async-start(), calls=%async_computation.2 | async-start | bytes 1048576 | tf_op jit(solution)/shard_map/psum | solution.py:18
  94.2 45.9 %copy-start.14 = (f32[256]{0:T(256)}, f32[256]{0:T(256)S(1)}, u32[]{:S(2)}) copy-start(f32[256]{0:T(256)S(1)} %dynamic-slice.3) | copy-start | bytes 3076
  122.7 17.4 %copy-start.11 = (bf16[48]{0:T(256)(128)(2,1)S(1)}, bf16[48]{0:T(256)(128)(2,1)}, u32[]{:S(2)}) copy-start(bf16[48]{0:T(256)(128)(2,1)} %copy-done.10) | copy-start | bytes 292
  139.1 3.7 copy-start.6
  149.7 1.9 copy-start.3
  149.8 2.8 copy-start.7
  163.5 4.2 collective-permute-start
  168.0 47.7 %collective-permute-start.1 = (f32[2,1024,256]{2,1,0:T(8,128)S(1)}, f32[2,1024,256]{2,1,0:T(8,128)S(1)}, u32[]{:S(2)}, u32[]{:S(2)}) collective-permute-start(f32[2,1024,256]{2,1,0:T(8,128)S(1)} %fusion.79), channel_id=1, source_target_pairs={{0,8},{4,12},{8,0},{12,4},{16,24},{20,28},{24,16},{28,20},{1,9},{5... | collective-permute-start | bytes 6291464 | tf_op jit(solution)/shard_map/ppermute | solution.py:11
  216.2 51.1 %copy-start.15 = (f32[256]{0:T(256)S(1)}, f32[256]{0:T(256)}, u32[]{:S(2)}) copy-start(f32[256]{0:T(256)} %copy-done.14) | copy-start | bytes 3076
  216.2 51.1 %copy-start.16 = (f32[256,256]{1,0:T(8,128)S(1)}, f32[256,256]{1,0:T(8,128)}, u32[]{:S(2)}) copy-start(f32[256,256]{1,0:T(8,128)} %reduce-scatter.2.cloned.1.call-done) | copy-start | bytes 786436
  216.2 47.0 %collective-permute-start.2 = (f32[2,1024,256]{2,1,0:T(8,128)S(1)}, f32[2,1024,256]{2,1,0:T(8,128)}, u32[]{:S(2)}, u32[]{:S(2)}) collective-permute-start(f32[2,1024,256]{2,1,0:T(8,128)S(1)} %fusion.89), channel_id=1, source_target_pairs={{0,16},{4,20},{8,24},{12,28},{16,0},{20,4},{24,8},{28,12},{1,17},{... | collective-permute-start | bytes 6291464 | tf_op jit(solution)/shard_map/ppermute | solution.py:11
  217.8 223.1 %copy-start.1 = (bf16[256,256]{1,0:T(8,128)(2,1)S(1)}, bf16[256,256]{1,0:T(8,128)(2,1)}, u32[]{:S(2)}) copy-start(bf16[256,256]{1,0:T(8,128)(2,1)} %param.10) | copy-start | bytes 393220
  265.4 172.1 %all-reduce.8.cloned.1.call-start = ((), (), s32[]{:S(2)}) async-start(), calls=%async_computation.3 | async-start | bytes 1048576 | tf_op jit(solution)/shard_map/psum | solution.py:77
  (1 other events, 1.9 us)
Sparse Core Ops, SparseCore 0:
  11.2 59.4 all-reduce.9
  94.1 26.5 reduce-scatter.1
  265.5 36.9 all-reduce.5
  308.4 129.1 all-reduce.7
